TPU v7x, 128 devices: a whole 4x4x4 slice. The times are simulated.
128 devices in a mesh: wide: 16 (over z_hi, x, core), narrow: 8 (over z_lo, y).
Axes of the slice: x: 4, y: 4, z: 4 (z_hi: 2, z_lo: 2; z = z_hi * 2 + z_lo), core: 2. Of those that a mesh axis runs over, the one named last changes fastest.
Arguments:
- tokens: bfloat16 [12288, 1024], P(('wide', 'narrow')), may hold values from -6 to 6
- cotangent: bfloat16 [12288, 1024], P(('wide', 'narrow')), may hold values from -6 to 6
- segments: int32 [16, 768], P('wide'), may hold values from 0 to 3, never falling along the last dimension, each value on 1 to 384 neighbouring positions
- w_query: bfloat16 [1024, 1024], P(None, 'narrow'), may hold values from -0.1875 to 0.1875
- w_key: bfloat16 [1024, 1024], P(None, 'narrow'), may hold values from -0.1875 to 0.1875
- w_value: bfloat16 [1024, 1024], P(None, 'narrow'), may hold values from -0.1875 to 0.1875
- w_out: bfloat16 [1024, 1024], P('narrow'), may hold values from -1.5 to 1.5
- w_gate: bfloat16 [1024, 4096], P(None, 'narrow'), may hold values from -0.1875 to 0.1875
- w_up: bfloat16 [1024, 4096], P(None, 'narrow'), may hold values from -0.1875 to 0.1875
- w_down: bfloat16 [4096, 1024], P('narrow'), may hold values from -0.09375 to 0.09375
- gain_one: float32 [1024], replicated, may hold values from 0.25 to 1.75
- bias_one: float32 [1024], replicated, may hold values from -2.5 to 2.5
- gain_two: float32 [1024], replicated, may hold values from 0.25 to 1.75
- bias_two: float32 [1024], replicated, may hold values from -2.5 to 2.5
Outputs:
- layer_out: float32 [12288, 1024], P(('wide', 'narrow'))
- input_grad: float32 [12288, 1024], P(('wide', 'narrow'))
- grad_query: float32 [1024, 1024], P(None, 'narrow')
- grad_key: float32 [1024, 1024], P(None, 'narrow')
- grad_value: float32 [1024, 1024], P(None, 'narrow')
- grad_out: float32 [1024, 1024], P('narrow')
- grad_gate: float32 [1024, 4096], P(None, 'narrow')
- grad_up: float32 [1024, 4096], P(None, 'narrow')
- grad_down: float32 [4096, 1024], P('narrow')
- grad_gain_one: float32 [1024], replicated
- grad_bias_one: float32 [1024], replicated
- grad_gain_two: float32 [1024], replicated
- grad_bias_two: float32 [1024], replicated
Inputs may be any that keep to these rules, and one draw needn't show every extreme that they name: `segments`: within each row of 768 tokens segment numbers never fall; each segment holds 1 to 384 tokens and one holds exactly 384.
All inputs are finite; a program needn't handle non-finite values.
Results may differ from a plain program's by a relative error of at most 0.03.
Values may be sent and summed in bfloat16 or wider, within the bound.
No kernel may reach another device: no remote copies, remote signals or barrier semaphores. Data moves between devices by JAX's collectives and lax.ppermute only.
A program may use at most 128 MiB of HBM per device.

v0:
```python
import math

import jax
import jax.numpy as jnp
from jax import lax
from jax.sharding import PartitionSpec as P

HD = 64


EPS = 1e-05
MASKED = -1e30


def normalize(values, gain_vec, bias_vec):
    centred = values - jnp.mean(values, axis=-1, keepdims=True)
    inverse = lax.rsqrt(jnp.mean(centred * centred, axis=-1, keepdims=True) + EPS)
    scaled = centred * inverse
    return (scaled * gain_vec + bias_vec, scaled, inverse)


def normalize_back(grad_in, scaled, inverse, gain_vec):
    along = grad_in * gain_vec
    return inverse * (
        along
        - jnp.mean(along, axis=-1, keepdims=True)
        - scaled * jnp.mean(along * scaled, axis=-1, keepdims=True)
    )


def contract_last(left_side, right_side):
    return lax.dot_general(
        left_side, right_side, (((1,), (1,)), ((), ())), preferred_element_type=jnp.float32
    )


def contract_first(left_side, right_side):
    return lax.dot_general(
        left_side, right_side, (((0,), (0,)), ((), ())), preferred_element_type=jnp.float32
    )


def rotary_tables(seg_rows):
    length = seg_rows.shape[-1]
    column = lax.broadcasted_iota(jnp.int32, (length, length), 1)
    row_index = lax.broadcasted_iota(jnp.int32, (length,), 0)
    same_segment = seg_rows[..., :, None] == seg_rows[..., None, :]
    first_index = jnp.min(jnp.where(same_segment, column, length), axis=-1)
    position = (row_index - first_index).astype(jnp.float32)
    half_width = HD // 2
    inverse = 10000.0 ** (-(2.0 * jnp.arange(half_width).astype(jnp.float32) / HD))
    angles = position[..., None] * inverse
    return (jnp.cos(angles), jnp.sin(angles), same_segment)


def rotate(values, cosine_table, sine_table):
    half_width = values.shape[-1] // 2
    first_half = values[..., :half_width]
    second_half = values[..., half_width:]
    cosine = cosine_table[..., None, :]
    sine_part = sine_table[..., None, :]
    return jnp.concatenate(
        [
            first_half * cosine - second_half * sine_part,
            second_half * cosine + first_half * sine_part,
        ],
        axis=-1,
    )


def unrotate(values, cosine_table, sine_table):
    half_width = values.shape[-1] // 2
    first_half = values[..., :half_width]
    second_half = values[..., half_width:]
    cosine = cosine_table[..., None, :]
    sine_part = sine_table[..., None, :]
    return jnp.concatenate(
        [
            first_half * cosine + second_half * sine_part,
            second_half * cosine - first_half * sine_part,
        ],
        axis=-1,
    )


def project_heads(normed_one, w_query, w_key, w_value, cosine_table, sine_table):
    row_count, length = (cosine_table.shape[0], cosine_table.shape[1])
    head_shape = (row_count, length, w_query.shape[1] // HD, HD)
    queries = rotate(
        jnp.dot(normed_one, w_query, preferred_element_type=jnp.float32).reshape(head_shape),
        cosine_table,
        sine_table,
    ).astype(jnp.bfloat16)
    key_rows = rotate(
        jnp.dot(normed_one, w_key, preferred_element_type=jnp.float32).reshape(head_shape),
        cosine_table,
        sine_table,
    ).astype(jnp.bfloat16)
    value_rows = (
        jnp.dot(normed_one, w_value, preferred_element_type=jnp.float32)
        .astype(jnp.bfloat16)
        .reshape(head_shape)
    )
    return (queries, key_rows, value_rows)


def attention_forward(normed_one, w_query, w_key, w_value, cosine_table, sine_table, same_segment):
    queries, key_rows, value_rows = project_heads(
        normed_one, w_query, w_key, w_value, cosine_table, sine_table
    )
    score_scale = 1.0 / math.sqrt(HD)

    def one_row(row_items):
        query_row, key_row, value_row, mask_row = row_items
        scores = (
            jnp.einsum("qhd,khd->hqk", query_row, key_row, preferred_element_type=jnp.float32)
            * score_scale
        )
        scores = jnp.where(mask_row[None], scores, MASKED)
        row_peak = jnp.max(scores, axis=-1, keepdims=True)
        exponent = jnp.exp(scores - row_peak)
        row_total = jnp.sum(exponent, axis=-1, keepdims=True)
        probs_low = (exponent / row_total).astype(jnp.bfloat16)
        output = jnp.einsum(
            "hqk,khd->qhd", probs_low, value_row, preferred_element_type=jnp.float32
        ).astype(jnp.bfloat16)
        return (output, row_peak + jnp.log(row_total))

    attended, log_total = lax.map(one_row, (queries, key_rows, value_rows, same_segment))
    return (attended.reshape(normed_one.shape[0], -1), log_total)


def attention_grads(
    normed_one,
    attended,
    log_total,
    branch_grad,
    w_query,
    w_key,
    w_value,
    w_out,
    cosine_table,
    sine_table,
    same_segment,
):
    queries, key_rows, value_rows = project_heads(
        normed_one, w_query, w_key, w_value, cosine_table, sine_table
    )
    score_scale = 1.0 / math.sqrt(HD)
    grad_out = contract_first(attended, branch_grad)
    attended_grad = contract_last(branch_grad, w_out).astype(jnp.bfloat16).reshape(queries.shape)

    def one_row(row_items):
        query_row, key_row, value_row, mask_row, total_row, grad_row = row_items
        scores = (
            jnp.einsum("qhd,khd->hqk", query_row, key_row, preferred_element_type=jnp.float32)
            * score_scale
        )
        scores = jnp.where(mask_row[None], scores, MASKED)
        probs = jnp.exp(scores - total_row)
        probs_low = probs.astype(jnp.bfloat16)
        prob_grad = jnp.einsum(
            "qhd,khd->hqk", grad_row, value_row, preferred_element_type=jnp.float32
        )
        score_grad = (
            probs * (prob_grad - jnp.sum(probs * prob_grad, axis=-1, keepdims=True))
        ).astype(jnp.bfloat16)
        query_grad = score_scale * jnp.einsum(
            "hqk,khd->qhd", score_grad, key_row, preferred_element_type=jnp.float32
        )
        key_grad = score_scale * jnp.einsum(
            "hqk,qhd->khd", score_grad, query_row, preferred_element_type=jnp.float32
        )
        value_grad = jnp.einsum(
            "hqk,qhd->khd", probs_low, grad_row, preferred_element_type=jnp.float32
        ).astype(jnp.bfloat16)
        return (query_grad, key_grad, value_grad)

    query_grad, key_grad, value_grad = lax.map(
        one_row, (queries, key_rows, value_rows, same_segment, log_total, attended_grad)
    )
    token_count = normed_one.shape[0]
    query_grad = (
        unrotate(query_grad, cosine_table, sine_table).astype(jnp.bfloat16).reshape(token_count, -1)
    )
    key_grad = (
        unrotate(key_grad, cosine_table, sine_table).astype(jnp.bfloat16).reshape(token_count, -1)
    )
    value_grad = value_grad.reshape(token_count, -1)
    grad_query = contract_first(normed_one, query_grad)
    grad_key = contract_first(normed_one, key_grad)
    grad_value = contract_first(normed_one, value_grad)
    partial_sum = (
        contract_last(query_grad, w_query)
        + contract_last(key_grad, w_key)
        + contract_last(value_grad, w_value)
    )
    return (partial_sum, grad_query, grad_key, grad_value, grad_out)


def swiglu(normed_two, w_gate, w_up):
    gate_pre = jnp.dot(normed_two, w_gate, preferred_element_type=jnp.float32)
    up_pre = jnp.dot(normed_two, w_up, preferred_element_type=jnp.float32)
    sigmoid_gate = jax.nn.sigmoid(gate_pre)
    active = gate_pre * sigmoid_gate
    hidden = (active * up_pre).astype(jnp.bfloat16)
    return (hidden, gate_pre, up_pre, sigmoid_gate, active)


def swiglu_grads(normed_two, out_grad, w_gate, w_up, w_down):
    hidden, gate_pre, up_pre, sigmoid_gate, active = swiglu(normed_two, w_gate, w_up)
    hidden_grad = contract_last(out_grad, w_down)
    grad_down = contract_first(hidden, out_grad)
    gate_grad = (
        hidden_grad * up_pre * sigmoid_gate * (1.0 + gate_pre * (1.0 - sigmoid_gate))
    ).astype(jnp.bfloat16)
    up_grad = (hidden_grad * active).astype(jnp.bfloat16)
    grad_gate = contract_first(normed_two, gate_grad)
    grad_up = contract_first(normed_two, up_grad)
    partial_sum = contract_last(gate_grad, w_gate) + contract_last(up_grad, w_up)
    return (partial_sum, grad_gate, grad_up, grad_down)


def per_device(
    tokens,
    cotangent,
    segments,
    w_query,
    w_key,
    w_value,
    w_out,
    w_gate,
    w_up,
    w_down,
    gain_one,
    bias_one,
    gain_two,
    bias_two,
):
    shard_rows = tokens.shape[0]
    narrow_index = lax.axis_index("narrow")
    cosine_table, sine_table, same_segment = rotary_tables(segments)
    gathered, cot_whole = (
        lax.all_gather(tokens, "narrow", axis=0, tiled=True),
        lax.all_gather(cotangent, "narrow", axis=0, tiled=True),
    )
    inputs = gathered.astype(jnp.float32)
    normed_float, scaled_one, inverse_one = normalize(inputs, gain_one, bias_one)
    normed_one = normed_float.astype(jnp.bfloat16)
    attended, log_total = attention_forward(
        normed_one, w_query, w_key, w_value, cosine_table, sine_table, same_segment
    )
    middle = inputs + lax.psum(
        jnp.dot(attended, w_out, preferred_element_type=jnp.float32).astype(jnp.bfloat16), "narrow"
    ).astype(jnp.float32)
    normed_float_two, scaled_two, inverse_two = normalize(middle, gain_two, bias_two)
    normed_two = normed_float_two.astype(jnp.bfloat16)
    hidden = swiglu(normed_two, w_gate, w_up)[0]
    result_whole = middle + lax.psum(
        jnp.dot(hidden, w_down, preferred_element_type=jnp.float32).astype(jnp.bfloat16), "narrow"
    ).astype(jnp.float32)
    layer_out = lax.dynamic_slice_in_dim(result_whole, narrow_index * shard_rows, shard_rows, 0)
    partial_two, grad_gate, grad_up, grad_down = swiglu_grads(
        normed_two, cot_whole, w_gate, w_up, w_down
    )
    normed_two_grad = lax.psum(partial_two.astype(jnp.bfloat16), "narrow").astype(jnp.float32)
    middle_grad = cot_whole.astype(jnp.float32) + normalize_back(
        normed_two_grad, scaled_two, inverse_two, gain_two
    )
    own_two_grad = lax.dynamic_slice_in_dim(
        normed_two_grad, narrow_index * shard_rows, shard_rows, 0
    )
    own_scaled_two = lax.dynamic_slice_in_dim(scaled_two, narrow_index * shard_rows, shard_rows, 0)
    branch_grad = middle_grad.astype(jnp.bfloat16)
    partial_one, grad_query, grad_key, grad_value, grad_out = attention_grads(
        normed_one,
        attended,
        log_total,
        branch_grad,
        w_query,
        w_key,
        w_value,
        w_out,
        cosine_table,
        sine_table,
        same_segment,
    )
    normed_one_grad = lax.psum(partial_one.astype(jnp.bfloat16), "narrow").astype(jnp.float32)
    input_whole = middle_grad + normalize_back(normed_one_grad, scaled_one, inverse_one, gain_one)
    input_grad = lax.dynamic_slice_in_dim(input_whole, narrow_index * shard_rows, shard_rows, 0)
    own_one_grad = lax.dynamic_slice_in_dim(
        normed_one_grad, narrow_index * shard_rows, shard_rows, 0
    )
    own_scaled_one = lax.dynamic_slice_in_dim(scaled_one, narrow_index * shard_rows, shard_rows, 0)
    matrices = (
        lax.psum(grad_query.astype(jnp.bfloat16), "wide").astype(jnp.float32),
        lax.psum(grad_key.astype(jnp.bfloat16), "wide").astype(jnp.float32),
        lax.psum(grad_value.astype(jnp.bfloat16), "wide").astype(jnp.float32),
        lax.psum(grad_out.astype(jnp.bfloat16), "wide").astype(jnp.float32),
        lax.psum(grad_gate.astype(jnp.bfloat16), "wide").astype(jnp.float32),
        lax.psum(grad_up.astype(jnp.bfloat16), "wide").astype(jnp.float32),
        lax.psum(grad_down.astype(jnp.bfloat16), "wide").astype(jnp.float32),
    )
    norm_grads = lax.psum(
        (
            jnp.sum(own_one_grad * own_scaled_one, axis=0),
            jnp.sum(own_one_grad, axis=0),
            jnp.sum(own_two_grad * own_scaled_two, axis=0),
            jnp.sum(own_two_grad, axis=0),
        ),
        ("wide", "narrow"),
    )
    return (
        layer_out,
        input_grad,
        matrices[0],
        matrices[1],
        matrices[2],
        matrices[3],
        matrices[4],
        matrices[5],
        matrices[6],
        norm_grads[0],
        norm_grads[1],
        norm_grads[2],
        norm_grads[3],
    )


def solution(mesh):
    placed = (
        P(("wide", "narrow"), None),
        P(("wide", "narrow"), None),
        P("wide", None),
        P(None, "narrow"),
        P(None, "narrow"),
        P(None, "narrow"),
        P("narrow", None),
        P(None, "narrow"),
        P(None, "narrow"),
        P("narrow", None),
        P(),
        P(),
        P(),
        P(),
    )
    return jax.shard_map(
        per_device,
        mesh=mesh,
        in_specs=placed,
        out_specs=(
            P(("wide", "narrow"), None),
            P(("wide", "narrow"), None),
            P(None, "narrow"),
            P(None, "narrow"),
            P(None, "narrow"),
            P("narrow", None),
            P(None, "narrow"),
            P(None, "narrow"),
            P("narrow", None),
            P(),
            P(),
            P(),
            P(),
        ),
        check_vma=False,
    )
```

profile of v0, /device:TPU:0, one launch (start us, length us, event | category | flops | bytes accessed | tf_op | source)
XLA Modules:
  0.0 550.6 jit_solution(14009956408082012891)
XLA Ops:
  10.9 41.9 %all-gather.3.cloned.1.call-done = bf16[768,1024]{1,0:T(8,128)(2,1)} async-done(((bf16[96,1024]{1,0:T(8,128)(2,1)}), bf16[768,1024]{1,0:T(8,128)(2,1)}) %all-gather.3.cloned.1.call-update) | async-done | bytes 1572880 | tf_op jit(solution)/shard_map/all_gather | solution.py:244
  54.6 2.0 fusion.4
  66.2 77.9 %all-reduce.8.cloned.1.call-done = bf16[768,1024]{1,0:T(8,128)(2,1)} async-done(((bf16[768,1024]{1,0:T(8,128)(2,1)}), bf16[768,1024]{1,0:T(8,128)(2,1)}) %all-reduce.8.cloned.1.call-update) | async-done | bytes 1572880 | tf_op jit(solution)/shard_map/psum | solution.py:253
  144.1 2.0 fusion.28
  146.9 3.6 add_convert_fusion.2
  150.4 2.1 fusion.32
  152.6 2.1 fusion.33
  154.7 31.3 %all-gather.5.cloned.1.call-done = bf16[768,1024]{1,0:T(8,128)(2,1)} async-done(((bf16[96,1024]{1,0:T(8,128)(2,1)}), bf16[768,1024]{1,0:T(8,128)(2,1)}) %all-gather.5.cloned.1.call-update) | async-done | bytes 1572880 | tf_op jit(solution)/shard_map/all_gather | solution.py:245
  185.9 5.0 multiply_convert_fusion.1
  192.7 2.2 add_convert_fusion.1
  195.2 3.3 convolution_convert_fusion
  198.4 75.3 %all-reduce.10.cloned.1.call-done = bf16[768,1024]{1,0:T(8,128)(2,1)} async-done(((bf16[768,1024]{1,0:T(8,128)(2,1)}), bf16[768,1024]{1,0:T(8,128)(2,1)}) %all-reduce.10.cloned.1.call-update) | async-done | bytes 1572880 | tf_op jit(solution)/shard_map/psum | solution.py:266
  273.7 3.2 multiply_reduce_fusion.4
  277.5 2.6 multiply_add_fusion
  288.8 3.7 convolution_convert_fusion.3
  292.6 2.0 convolution_convert_fusion.4
  294.6 2.0 convolution_convert_fusion.2
  301.8 3.4 convert_element_type.182
  305.2 73.7 %all-reduce.14.cloned.1.call-done = (bf16[768,1024]{1,0:T(8,128)(2,1)}, bf16[768,1024]{1,0:T(8,128)(2,1)}) async-done(((bf16[768,1024]{1,0:T(8,128)(2,1)}, bf16[768,1024]{1,0:T(8,128)(2,1)}), (bf16[768,1024]{1,0:T(8,128)(2,1)}, bf16[768,1024]{1,0:T(8,128)(2,1)})) %all-reduce.14.cloned.1.call-update) | async-done | bytes 3145744 | tf_op jit(solution)/shard_map/psum | solution.py:259
  378.9 1.9 convert_element_type.192
  382.2 2.2 dynamic-slice_reduce_fusion
  384.4 65.4 %all-reduce = (f32[1024]{0:T(1024)}, f32[1024]{0:T(1024)}, f32[1024]{0:T(1024)}, f32[1024]{0:T(1024)}) all-reduce(f32[1024]{0:T(1024)S(1)} %get-tuple-element.113, f32[1024]{0:T(1024)S(1)} %get-tuple-element.114, f32[1024]{0:T(1024)S(1)} %get-tuple-element.55, ...), channel_id=1, replica_groups=mesh['wide'=16,'narrow'=8] {'wide','narrow'}, use_global_device_ids=true, to_apply=%region_24.25 | all-reduce | flops 4096 | bytes 32768 | tf_op jit(solution)/shard_map/psum | solution.py:304
  451.6 82.6 %all-reduce.12.cloned.1.call-done = (bf16[1024,128]{1,0:T(8,128)(2,1)}, bf16[1024,128]{1,0:T(8,128)(2,1)}, bf16[1024,128]{1,0:T(8,128)(2,1)}, bf16[128,1024]{1,0...) async-done(((bf16[1024,128]{1,0:T(8,128)(2,1)}, bf16[1024,128]{1,0:T(8,128)(2,1)}, bf16[1024,128]{1,0:T(8,128)(2,1)}, ...) | async-done | bytes 4194320 | tf_op jit(solution)/shard_map/psum | solution.py:296
  534.2 3.0 convert_element_type.202
  (177 shorter events, 41.7 us)
Async XLA Ops:
  7.2 178.8 %copy-start = (bf16[512,1024]{1,0:T(8,128)(2,1)S(1)}, bf16[512,1024]{1,0:T(8,128)(2,1)}, u32[]{:S(2)}) copy-start(bf16[512,1024]{1,0:T(8,128)(2,1)} %param.23) | copy-start | bytes 3145732
  7.2 49.4 %copy-start.49 = (f32[1024]{0:T(1024)S(1)}, f32[1024]{0:T(1024)}, u32[]{:S(2)}) copy-start(f32[1024]{0:T(1024)} %param.24) | copy-start | bytes 12292
  7.2 49.4 %copy-start.50 = (f32[1024]{0:T(1024)S(1)}, f32[1024]{0:T(1024)}, u32[]{:S(2)}) copy-start(f32[1024]{0:T(1024)} %param.25) | copy-start | bytes 12292
  7.2 45.6 %all-gather.3.cloned.1.call-start = ((), (), s32[]{:S(2)}) async-start(), calls=%async_computation | async-start | bytes 1769472 | tf_op jit(solution)/shard_map/all_gather | solution.py:244
  8.0 136.2 %all-reduce.8.cloned.1.call-start = ((), (), s32[]{:S(2)}) async-start(), calls=%async_computation.1 | async-start | bytes 3145728 | tf_op jit(solution)/shard_map/psum | solution.py:253
  9.7 49.7 %copy-start.26 = (f32[768,32]{0,1:T(8,128)}, f32[768,32]{0,1:T(8,128)S(1)}, u32[]{:S(2)}) copy-start(f32[768,32]{0,1:T(8,128)S(1)} %get-tuple-element.107) | copy-start | bytes 294916
  10.9 46.4 %copy-start.22 = (bf16[1024,128]{1,0:T(8,128)(2,1)S(1)}, bf16[1024,128]{1,0:T(8,128)(2,1)}, u32[]{:S(2)}) copy-start(bf16[1024,128]{1,0:T(8,128)(2,1)} %param.17) | copy-start | bytes 786436
  52.8 3.9 copy-start.2
  65.2 120.7 %all-gather.5.cloned.1.call-start = ((), (), s32[]{:S(2)}) async-start(), calls=%async_computation.2 | async-start | bytes 1769472 | tf_op jit(solution)/shard_map/all_gather | solution.py:245
  66.0 80.9 %copy-start.48 = (f32[1024]{0:T(1024)S(1)}, f32[1024]{0:T(1024)}, u32[]{:S(2)}) copy-start(f32[1024]{0:T(1024)} %param.26) | copy-start | bytes 12292
  66.0 80.9 %copy-start.51 = (f32[1024]{0:T(1024)S(1)}, f32[1024]{0:T(1024)}, u32[]{:S(2)}) copy-start(f32[1024]{0:T(1024)} %param.27) | copy-start | bytes 12292
  66.0 207.7 %all-reduce.10.cloned.1.call-start = ((), (), s32[]{:S(2)}) async-start(), calls=%async_computation.3 | async-start | bytes 3145728 | tf_op jit(solution)/shard_map/psum | solution.py:266
  185.9 5.0 copy-start.16
  194.9 184.0 %all-reduce.14.cloned.1.call-start = ((), (), s32[]{:S(2)}) async-start(), calls=%async_computation.5 | async-start | bytes 6291456 | tf_op jit(solution)/shard_map/psum | solution.py:259
  273.7 3.8 copy-start.9
  273.7 7.0 %slice-start = ((s8[4718592]{0:T(1024)(128)(4,1)}), s8[4194304]{0:T(1024)(128)(4,1)S(1)}, s32[]{:S(2)}) async-start(s8[4718592]{0:T(1024)(128)(4,1)} %bitcast.74), calls=%async_computation.6 | async-start | bytes 8388608
  288.5 4.1 copy-start.29
  288.5 245.7 %all-reduce.12.cloned.1.call-start = ((), (), s32[]{:S(2)}) async-start(), calls=%async_computation.4 | async-start | bytes 8388608 | tf_op jit(solution)/shard_map/psum | solution.py:296
  296.6 4.0 copy-start.7
  296.6 4.0 copy-start.32
  534.2 4.6 copy-start.19
  537.2 4.0 copy-start.46
  538.8 4.1 copy-start.44
  538.8 4.9 copy-start.1
  (37 other events, 73.3 us)
Sparse Core Ops, SparseCore 0:
  9.7 43.0 all-gather.2
  65.4 78.7 all-reduce.7
  145.8 40.1 all-gather.4
  195.0 78.6 all-reduce.9
  288.6 90.2 all-reduce.13
  382.4 151.7 all-reduce.11
where the time goes:
time: 551 us
  waiting for transfers between devices  384 us (70%)
  blocking collectives  65.4 us (12%)
  other arithmetic  41.2 us (7%)
  matrix products  41 us (7%)
  between operations  14.8 us (3%)
    psum x1, waiting for transfers between devices, per_device(): lax.psum(grad_query.astype(jnp.bfloat16), 'wide').astype(jnp.float32)  82.6 us
    psum x1, waiting for transfers between devices, per_device(): lax.psum(jnp.dot(attended, w_out, preferred_element_type=jnp.float32).ast...  77.9 us
    psum x1, waiting for transfers between devices, per_device(): lax.psum(partial_two.astype(jnp.bfloat16), 'narrow').astype(jnp.float32)  75.3 us
    psum x1, waiting for transfers between devices, per_device(): lax.psum(jnp.dot(hidden, w_down, preferred_element_type=jnp.float32).asty...  73.7 us
    psum x1, blocking collectives, per_device(): lax.psum((jnp.sum(own_one_grad * own_scaled_one, axis=0), jnp.sum(own_one...  65.4 us
    all_gather x1, waiting for transfers between devices, per_device(): lax.all_gather(tokens, 'narrow', axis=0, tiled=True)  41.9 us
    all_gather x1, waiting for transfers between devices, per_device(): lax.all_gather(cotangent, 'narrow', axis=0, tiled=True)  31.3 us
    dot_general x7, matrix products, contract_first(): lax.dot_general(left_side, right_side, (((0,), (0,)), ((), ())), preferre...  12.8 us
  transfers between devices with their start and end apart: 6, of which 6 were waited for; matrix products, arithmetic and copies ran while one was open for 7% of the time, Pallas kernels for 0%

commit v1 on v0

v1 whole, which is shorter than its diff:
```python
import math

import jax
import jax.numpy as jnp
from jax import lax
from jax.sharding import PartitionSpec as P

HD = 64
EPS = 1e-05
MASKED = -1e30
F32 = jnp.float32
BF16 = jnp.bfloat16


def normalize(values, gain_vec, bias_vec):
    centred = values - jnp.mean(values, axis=-1, keepdims=True)
    inverse = lax.rsqrt(jnp.mean(centred * centred, axis=-1, keepdims=True) + EPS)
    scaled = centred * inverse
    return (scaled * gain_vec + bias_vec, scaled, inverse)


def normalize_back(grad_in, scaled, inverse, gain_vec):
    along = grad_in * gain_vec
    return inverse * (
        along
        - jnp.mean(along, axis=-1, keepdims=True)
        - scaled * jnp.mean(along * scaled, axis=-1, keepdims=True)
    )


def contract_last(left_side, right_side):
    return lax.dot_general(
        left_side, right_side, (((1,), (1,)), ((), ())), preferred_element_type=F32
    )


def contract_first(left_side, right_side):
    return lax.dot_general(
        left_side, right_side, (((0,), (0,)), ((), ())), preferred_element_type=F32
    )


def rotate(values, cosine_table, sine_table):
    half_width = values.shape[-1] // 2
    first_half = values[..., :half_width]
    second_half = values[..., half_width:]
    cosine = cosine_table[:, None, :]
    sine_part = sine_table[:, None, :]
    return jnp.concatenate(
        [
            first_half * cosine - second_half * sine_part,
            second_half * cosine + first_half * sine_part,
        ],
        axis=-1,
    )


def unrotate(values, cosine_table, sine_table):
    half_width = values.shape[-1] // 2
    first_half = values[..., :half_width]
    second_half = values[..., half_width:]
    cosine = cosine_table[:, None, :]
    sine_part = sine_table[:, None, :]
    return jnp.concatenate(
        [
            first_half * cosine + second_half * sine_part,
            second_half * cosine - first_half * sine_part,
        ],
        axis=-1,
    )


def roll_blocks(values, shift_rows):
    doubled = jnp.concatenate([values, values], axis=0)
    return lax.dynamic_slice_in_dim(doubled, shift_rows, values.shape[0], 0)


def narrow_gather(own, count):
    pieces = [own]
    for k in range(1, count):
        pieces.append(
            lax.ppermute(own, "narrow", [((i + k) % count, i) for i in range(count)])
        )
    return jnp.concatenate(pieces, axis=0)


def narrow_scatter(partial, count):
    blocks = partial.reshape(count, partial.shape[0] // count, partial.shape[1])
    total = blocks[0].astype(F32)
    for k in range(1, count):
        total = total + lax.ppermute(
            blocks[k], "narrow", [(i, (i + k) % count) for i in range(count)]
        ).astype(F32)
    return total


def wide_perm(mapping, wide):
    return [(w, mapping(w)) for w in range(wide)]


def wide_allreduce(grads, wide):
    chips_x = wide // 4
    w = lax.axis_index("wide")
    core = w % 2
    xpos = (w // 2) % chips_x
    zhi = w // (2 * chips_x)

    def to_core(v):
        return v ^ 1

    def to_x(k):
        def mapping(v):
            c, xx, zz = v % 2, (v // 2) % chips_x, v // (2 * chips_x)
            return zz * 2 * chips_x + ((xx + k) % chips_x) * 2 + c

        return mapping

    def to_z(v):
        c, xx, zz = v % 2, (v // 2) % chips_x, v // (2 * chips_x)
        return (1 - zz) * 2 * chips_x + xx * 2 + c

    results = []
    for g in grads:
        rows, cols = g.shape
        half = rows // 2
        parts = g.reshape(2, half, cols)
        keep = lax.dynamic_index_in_dim(parts, core, 0, keepdims=False)
        send = lax.dynamic_index_in_dim(parts, 1 - core, 0, keepdims=False)
        summed = keep.astype(F32) + lax.ppermute(send, "wide", wide_perm(to_core, wide)).astype(F32)
        quarter = half // chips_x
        quarters = summed.reshape(chips_x, quarter, cols)
        acc = lax.dynamic_index_in_dim(quarters, xpos, 0, keepdims=False)
        for k in range(1, chips_x):
            piece = lax.dynamic_index_in_dim(quarters, (xpos + k) % chips_x, 0, keepdims=False)
            acc = acc + lax.ppermute(
                piece.astype(BF16), "wide", wide_perm(to_x(k), wide)
            ).astype(F32)
        eighth = quarter // 2
        eighths = acc.reshape(2, eighth, cols)
        mine = lax.dynamic_index_in_dim(eighths, zhi, 0, keepdims=False)
        other = lax.dynamic_index_in_dim(eighths, 1 - zhi, 0, keepdims=False)
        final = (mine + lax.ppermute(other.astype(BF16), "wide", wide_perm(to_z, wide)).astype(F32)).astype(BF16)
        got = lax.ppermute(final, "wide", wide_perm(to_z, wide))
        pair = jnp.concatenate([final, got], axis=0)
        pair = roll_blocks(pair, zhi * eighth)
        pieces = [pair]
        for k in range(1, chips_x):
            pieces.append(
                lax.ppermute(pair, "wide", [(to_x(k)(v), v) for v in range(wide)])
            )
        ring = jnp.concatenate(pieces, axis=0)
        halfrow = roll_blocks(ring, ((chips_x - xpos) % chips_x) * quarter)
        partner = lax.ppermute(halfrow, "wide", wide_perm(to_core, wide))
        whole = jnp.concatenate([halfrow, partner], axis=0)
        whole = roll_blocks(whole, core * half)
        results.append(whole.astype(F32))
    return results


def per_device(
    tokens,
    cotangent,
    segments,
    w_query,
    w_key,
    w_value,
    w_out,
    w_gate,
    w_up,
    w_down,
    gain_one,
    bias_one,
    gain_two,
    bias_two,
):
    count = lax.axis_size("narrow")
    wide = lax.axis_size("wide")
    block = tokens.shape[0]
    narrow_index = lax.axis_index("narrow")
    shift = narrow_index * block

    seg = segments[0]
    length = seg.shape[0]
    column = lax.broadcasted_iota(jnp.int32, (length, length), 1)
    same_orig = seg[:, None] == seg[None, :]
    first_index = jnp.min(jnp.where(same_orig, column, length), axis=-1)
    position = jnp.arange(length, dtype=jnp.int32) - first_index
    seg_rot = roll_blocks(seg, shift)
    pos_rot = roll_blocks(position, shift).astype(F32)
    same_segment = seg_rot[:, None] == seg_rot[None, :]
    inverse = 10000.0 ** (-(2.0 * jnp.arange(HD // 2).astype(F32) / HD))
    angles = pos_rot[:, None] * inverse
    cosine_table, sine_table = jnp.cos(angles), jnp.sin(angles)

    tok_full = narrow_gather(tokens, count)
    cot_full = narrow_gather(cotangent, count)

    inputs = tok_full.astype(F32)
    normed_float, scaled_one, inverse_one = normalize(inputs, gain_one, bias_one)
    normed_one = normed_float.astype(BF16)
    own_scaled_one = scaled_one[:block]
    own_inverse_one = inverse_one[:block]

    heads = w_query.shape[1] // HD
    head_shape = (length, heads, HD)
    queries = rotate(
        jnp.dot(normed_one, w_query, preferred_element_type=F32).reshape(head_shape),
        cosine_table,
        sine_table,
    ).astype(BF16)
    key_rows = rotate(
        jnp.dot(normed_one, w_key, preferred_element_type=F32).reshape(head_shape),
        cosine_table,
        sine_table,
    ).astype(BF16)
    value_rows = (
        jnp.dot(normed_one, w_value, preferred_element_type=F32).astype(BF16).reshape(head_shape)
    )
    score_scale = 1.0 / math.sqrt(HD)
    scores = (
        jnp.einsum("qhd,khd->hqk", queries, key_rows, preferred_element_type=F32) * score_scale
    )
    scores = jnp.where(same_segment[None], scores, MASKED)
    row_peak = jnp.max(scores, axis=-1, keepdims=True)
    exponent = jnp.exp(scores - row_peak)
    row_total = jnp.sum(exponent, axis=-1, keepdims=True)
    probs = exponent / row_total
    probs_low = probs.astype(BF16)
    attended = (
        jnp.einsum("hqk,khd->qhd", probs_low, value_rows, preferred_element_type=F32)
        .astype(BF16)
        .reshape(length, -1)
    )

    branch_partial = jnp.dot(attended, w_out, preferred_element_type=F32).astype(BF16)
    branch_own = narrow_scatter(branch_partial, count)
    middle_own = tokens.astype(F32) + branch_own
    normed_two_float, scaled_two, inverse_two = normalize(middle_own, gain_two, bias_two)
    normed_two = narrow_gather(normed_two_float.astype(BF16), count)

    gate_pre = jnp.dot(normed_two, w_gate, preferred_element_type=F32)
    up_pre = jnp.dot(normed_two, w_up, preferred_element_type=F32)
    sigmoid_gate = jax.nn.sigmoid(gate_pre)
    active = gate_pre * sigmoid_gate
    hidden = (active * up_pre).astype(BF16)
    ffn_partial = jnp.dot(hidden, w_down, preferred_element_type=F32).astype(BF16)
    layer_out = middle_own + narrow_scatter(ffn_partial, count)

    hidden_grad = contract_last(cot_full, w_down)
    grad_down = contract_first(hidden, cot_full)
    gate_grad = (
        hidden_grad * up_pre * sigmoid_gate * (1.0 + gate_pre * (1.0 - sigmoid_gate))
    ).astype(BF16)
    up_grad = (hidden_grad * active).astype(BF16)
    grad_gate = contract_first(normed_two, gate_grad)
    grad_up = contract_first(normed_two, up_grad)
    two_partial = (contract_last(gate_grad, w_gate) + contract_last(up_grad, w_up)).astype(BF16)
    ffn_grads = wide_allreduce(
        [grad_gate.astype(BF16), grad_up.astype(BF16), grad_down.astype(BF16)], wide
    )

    own_two_grad = narrow_scatter(two_partial, count)
    middle_grad = cotangent.astype(F32) + normalize_back(
        own_two_grad, scaled_two, inverse_two, gain_two
    )
    branch_grad = narrow_gather(middle_grad.astype(BF16), count)

    grad_out = contract_first(attended, branch_grad)
    attended_grad = contract_last(branch_grad, w_out).astype(BF16).reshape(head_shape)
    prob_grad = jnp.einsum(
        "qhd,khd->hqk", attended_grad, value_rows, preferred_element_type=F32
    )
    score_grad = (
        probs * (prob_grad - jnp.sum(probs * prob_grad, axis=-1, keepdims=True))
    ).astype(BF16)
    query_grad = score_scale * jnp.einsum(
        "hqk,khd->qhd", score_grad, key_rows, preferred_element_type=F32
    )
    key_grad = score_scale * jnp.einsum(
        "hqk,qhd->khd", score_grad, queries, preferred_element_type=F32
    )
    value_grad = jnp.einsum(
        "hqk,qhd->khd", probs_low, attended_grad, preferred_element_type=F32
    ).astype(BF16).reshape(length, -1)
    query_grad = unrotate(query_grad, cosine_table, sine_table).astype(BF16).reshape(length, -1)
    key_grad = unrotate(key_grad, cosine_table, sine_table).astype(BF16).reshape(length, -1)
    grad_query = contract_first(normed_one, query_grad)
    grad_key = contract_first(normed_one, key_grad)
    grad_value = contract_first(normed_one, value_grad)
    one_partial = (
        contract_last(query_grad, w_query)
        + contract_last(key_grad, w_key)
        + contract_last(value_grad, w_value)
    ).astype(BF16)
    attn_grads = wide_allreduce(
        [
            grad_query.astype(BF16),
            grad_key.astype(BF16),
            grad_value.astype(BF16),
            grad_out.astype(BF16),
        ],
        wide,
    )
    own_one_grad = narrow_scatter(one_partial, count)
    input_grad = middle_grad + normalize_back(
        own_one_grad, own_scaled_one, own_inverse_one, gain_one
    )
    norm_grads = lax.psum(
        (
            jnp.sum(own_one_grad * own_scaled_one, axis=0),
            jnp.sum(own_one_grad, axis=0),
            jnp.sum(own_two_grad * scaled_two, axis=0),
            jnp.sum(own_two_grad, axis=0),
        ),
        ("wide", "narrow"),
    )
    return (
        layer_out,
        input_grad,
        attn_grads[0],
        attn_grads[1],
        attn_grads[2],
        attn_grads[3],
        ffn_grads[0],
        ffn_grads[1],
        ffn_grads[2],
        norm_grads[0],
        norm_grads[1],
        norm_grads[2],
        norm_grads[3],
    )


def solution(mesh):
    placed = (
        P(("wide", "narrow"), None),
        P(("wide", "narrow"), None),
        P("wide", None),
        P(None, "narrow"),
        P(None, "narrow"),
        P(None, "narrow"),
        P("narrow", None),
        P(None, "narrow"),
        P(None, "narrow"),
        P("narrow", None),
        P(),
        P(),
        P(),
        P(),
    )
    return jax.shard_map(
        per_device,
        mesh=mesh,
        in_specs=placed,
        out_specs=(
            P(("wide", "narrow"), None),
            P(("wide", "narrow"), None),
            P(None, "narrow"),
            P(None, "narrow"),
            P(None, "narrow"),
            P("narrow", None),
            P(None, "narrow"),
            P(None, "narrow"),
            P("narrow", None),
            P(),
            P(),
            P(),
            P(),
        ),
        check_vma=False,
    )
```

time: 551 us -> 504 us (0.915); the launches traced: 551 us -> 497 us
  waiting for transfers between devices: 384 us -> 148 us
  starting transfers between devices: 0.9 us -> 181 us
  local copies, waits for them, and re-layouts: 3.24 us -> 31.2 us
  between operations: 14.8 us -> 2.53 us
  matrix products: 41 us -> 29 us
    psum x4 -> x0, waiting for transfers between devices: 309 us -> none  [the longest x1 82.6 us: per_device(): lax.psum(grad_query.astype(jnp.bfloat16), 'wide').astype(jnp.float32)]
    ppermute x0 -> x126, starting transfers between devices: none -> 181 us  [the longest x28 49.6 us: narrow_scatter(): lax.ppermute(blocks[k], 'narrow', [(i, (i + k) % count) for i in range(co...]
    ppermute x0 -> x126, waiting for transfers between devices: none -> 148 us  [the longest x21 40.7 us: wide_allreduce(): lax.ppermute(pair, 'wide', [(to_x(k)(v), v) for v in range(wide)])]
    all_gather x2 -> x0, waiting for transfers between devices: 73.1 us -> none  [the longest x1 41.9 us: per_device(): lax.all_gather(tokens, 'narrow', axis=0, tiled=True)]
    unnamed x110 -> x134, local copies, waits for them, and re-layouts: 3.01 us -> 23.1 us
    dot_general x7, matrix products: 12.8 us -> 5.27 us  [contract_first(): lax.dot_general(left_side, right_side, (((0,), (0,)), ((), ())), preferre...]
    dot_general x7, matrix products: 11.7 us -> 6.18 us  [contract_last(): lax.dot_general(left_side, right_side, (((1,), (1,)), ((), ())), preferre...]
    dot_general x13 -> x12, matrix products: 16.5 us -> 12.3 us  [the longest x1 3.03 us: per_device(): jnp.einsum('hqk,khd->qhd', probs_low, value_rows, preferred_element_type=...]
  transfers between devices with their start and end apart: 6 -> 126, of which waited for: 6 -> 53; matrix products, arithmetic and copies ran while one was open for 7% -> 18% of each run, Pallas kernels for 0% -> 0%
where the time goes in v1:
time: 504 us; the launch traced here: 497 us
  starting transfers between devices  181 us (36%)
  waiting for transfers between devices  148 us (29%)
  blocking collectives  62.9 us (12%)
  other arithmetic  41.5 us (8%)
  local copies, waits for them, and re-layouts  31.2 us (6%)
  matrix products  29 us (6%)
    psum x1, blocking collectives, per_device(): lax.psum((jnp.sum(own_one_grad * own_scaled_one, axis=0), jnp.sum(own_one...  62.9 us
    ppermute x28, starting transfers between devices, narrow_scatter(): lax.ppermute(blocks[k], 'narrow', [(i, (i + k) % count) for i in range(co...  49.6 us
    ppermute x28, starting transfers between devices, narrow_gather(): lax.ppermute(own, 'narrow', [((i + k) % count, i) for i in range(count)])  47.3 us
    ppermute x21, waiting for transfers between devices, wide_allreduce(): lax.ppermute(pair, 'wide', [(to_x(k)(v), v) for v in range(wide)])  40.7 us
    ppermute x28, waiting for transfers between devices, narrow_gather(): lax.ppermute(own, 'narrow', [((i + k) % count, i) for i in range(count)])  34.6 us
    ppermute x7, waiting for transfers between devices, wide_allreduce(): lax.ppermute(other.astype(BF16), 'wide', wide_perm(to_z, wide)).astype(F32)  30.1 us
    ppermute x21, starting transfers between devices, wide_allreduce(): lax.ppermute(piece.astype(BF16), 'wide', wide_perm(to_x(k), wide))  29.2 us
    ppermute x21, starting transfers between devices, wide_allreduce(): lax.ppermute(pair, 'wide', [(to_x(k)(v), v) for v in range(wide)])  25.9 us
  transfers between devices with their start and end apart: 126, of which 53 were waited for; matrix products, arithmetic and copies ran while one was open for 18% of the time, Pallas kernels for 0%

profile of v1, /device:TPU:0, one launch (start us, length us, event | category | flops | bytes accessed | tf_op | source)
XLA Modules:
  0.0 496.7 jit_solution(448274569098398275)
XLA Ops:
  0.7 4.5 collective-permute-start
  22.7 4.7 collective-permute-start.29
  39.3 5.3 %fusion.146 = (f32[2,768]{1,0:T(2,128)S(1)}, f32[2,768,768]{1,2,0:T(8,128)}) fusion(pred[768,768]{0,1:T(8,128)(4,1)} %broadcast_compare_fusion, bf16[768,2,32]{0,2,1:T(8,128)(2,1)} %get-tuple-element.112, bf16[768,2,32]{0,2,1:T(8,128)(2,1)} %get-tuple-element.113, bf16[768,2,32]{0,2,1:T(8,128)(2,1)} %get-tuple-element.95, ...), kind=kOutput, calls=%fused_computation.411 | convolution fusion | flops 156500736 | bytes 5707776 | tf_op jit(solution)/shard_map/sub | solution.py:225
  62.4 5.3 %collective-permute-start.7 = (bf16[96,1024]{1,0:T(8,128)(2,1)S(1)}, bf16[96,1024]{1,0:T(8,128)(2,1)S(1)}, u32[]{:S(2)}, u32[]{:S(2)}) collective-permute-start(bf16[96,1024]{1,0:T(8,128)(2,1)S(1)} %get-tuple-element.74), channel_id=1, source_target_pairs={{0,1},{1,2},{2,3},{3,4},{4,5},{5,6},{6,7},{7,0},{8,9},{9,10},{10,1... | collective-permute-start | bytes 589832 | tf_op jit(solution)/shard_map/ppermute | solution.py:91
  70.3 9.8 %collective-permute-done.10 = bf16[96,1024]{1,0:T(8,128)(2,1)S(1)} collective-permute-done((bf16[96,1024]{1,0:T(8,128)(2,1)S(1)}, bf16[96,1024]{1,0:T(8,128)(2,1)S(1)}, u32[]{:S(2)}, u32[]{:S(2)}) %collective-permute-start.10) | collective-permute-done | bytes 196640 | tf_op jit(solution)/shard_map/ppermute | solution.py:91
  81.0 4.2 collective-permute-start.14
  85.3 6.3 %collective-permute-done.34 = bf16[96,1024]{1,0:T(8,128)(2,1)S(1)} collective-permute-done((bf16[96,1024]{1,0:T(8,128)(2,1)}, bf16[96,1024]{1,0:T(8,128)(2,1)S(1)}, u32[]{:S(2)}, u32[]{:S(2)}) %collective-permute-start.34) | collective-permute-done | bytes 196640 | tf_op jit(solution)/shard_map/ppermute | solution.py:82
  99.6 4.2 collective-permute-done.19
  122.4 4.8 collective-permute-done.41
  127.2 6.4 %collective-permute-start.35 = (bf16[96,1024]{1,0:T(8,128)(2,1)S(1)}, bf16[96,1024]{1,0:T(8,128)(2,1)S(1)}, u32[]{:S(2)}, u32[]{:S(2)}) collective-permute-start(bf16[96,1024]{1,0:T(8,128)(2,1)S(1)} %get-tuple-element.60), channel_id=1, source_target_pairs={{0,1},{1,2},{2,3},{3,4},{4,5},{5,6},{6,7},{7,0},{8,9},{9,10},{10,1... | collective-permute-start | bytes 589832 | tf_op jit(solution)/shard_map/ppermute | solution.py:91
  135.2 4.7 collective-permute-start.26
  164.3 5.4 %collective-permute-done.44 = bf16[96,1024]{1,0:T(8,128)(2,1)S(1)} collective-permute-done((bf16[96,1024]{1,0:T(8,128)(2,1)S(1)}, bf16[96,1024]{1,0:T(8,128)(2,1)S(1)}, u32[]{:S(2)}, u32[]{:S(2)}) %collective-permute-start.44) | collective-permute-done | bytes 196640 | tf_op jit(solution)/shard_map/ppermute | solution.py:82
  174.9 4.4 collective-permute-done.46
  182.0 5.1 %collective-permute-done.48 = bf16[96,1024]{1,0:T(8,128)(2,1)S(1)} collective-permute-done((bf16[96,1024]{1,0:T(8,128)(2,1)S(1)}, bf16[96,1024]{1,0:T(8,128)(2,1)S(1)}, u32[]{:S(2)}, u32[]{:S(2)}) %collective-permute-start.48) | collective-permute-done | bytes 196640 | tf_op jit(solution)/shard_map/ppermute | solution.py:82
  230.2 4.1 collective-permute-start.60
  244.9 5.9 %collective-permute-done.80 = bf16[64,128]{1,0:T(8,128)(2,1)S(1)} collective-permute-done((bf16[64,128]{1,0:T(8,128)(2,1)S(1)}, bf16[64,128]{1,0:T(8,128)(2,1)S(1)}, u32[]{:S(2)}, u32[]{:S(2)}) %collective-permute-start.80) | collective-permute-done | bytes 16416 | tf_op jit(solution)/shard_map/ppermute | solution.py:142
  252.0 4.8 collective-permute-done.90
  291.2 62.9 %all-reduce = (f32[1024]{0:T(1024)}, f32[1024]{0:T(1024)}, f32[1024]{0:T(1024)}, f32[1024]{0:T(1024)}) all-reduce(f32[1024]{0:T(1024)S(1)} %get-tuple-element.13, f32[1024]{0:T(1024)} %get-tuple-element.20, f32[1024]{0:T(1024)S(1)} %get-tuple-element.15, ...), channel_id=1, replica_groups=mesh['wide'=16,'narrow'=8] {'wide','narrow'}, use_global_device_ids=true, to_apply=%region_13.14 | all-reduce | flops 4096 | bytes 32768 | tf_op jit(solution)/shard_map/psum | solution.py:308
  370.2 4.7 collective-permute-done.73
  375.8 4.7 collective-permute-done.74
  390.3 4.2 collective-permute-done.83
  441.8 4.3 collective-permute-done.120
  484.9 4.1 fusion.32
  489.0 4.1 fusion.28
  (502 shorter events, 315.2 us)
Async XLA Ops:
  21.2 27.2 %collective-permute-start.28 = (bf16[96,1024]{1,0:T(8,128)(2,1)}, bf16[96,1024]{1,0:T(8,128)(2,1)}, u32[]{:S(2)}, u32[]{:S(2)}) collective-permute-start(bf16[96,1024]{1,0:T(8,128)(2,1)} %param.15), channel_id=1, source_target_pairs={{1,0},{2,1},{3,2},{4,3},{5,4},{6,5},{7,6},{0,7},{9,8},{10,9},{11,1... | collective-permute-start | bytes 589832 | tf_op jit(solution)/shard_map/ppermute | solution.py:82
  22.7 29.1 %collective-permute-start.29 = (bf16[96,1024]{1,0:T(8,128)(2,1)}, bf16[96,1024]{1,0:T(8,128)(2,1)}, u32[]{:S(2)}, u32[]{:S(2)}) collective-permute-start(bf16[96,1024]{1,0:T(8,128)(2,1)} %param.15), channel_id=1, source_target_pairs={{2,0},{3,1},{4,2},{5,3},{6,4},{7,5},{0,6},{1,7},{10,8},{11,9},{12,... | collective-permute-start | bytes 589832 | tf_op jit(solution)/shard_map/ppermute | solution.py:82
  27.5 26.5 %collective-permute-start.30 = (bf16[96,1024]{1,0:T(8,128)(2,1)}, bf16[96,1024]{1,0:T(8,128)(2,1)}, u32[]{:S(2)}, u32[]{:S(2)}) collective-permute-start(bf16[96,1024]{1,0:T(8,128)(2,1)} %param.15), channel_id=1, source_target_pairs={{3,0},{4,1},{5,2},{6,3},{7,4},{0,5},{1,6},{2,7},{11,8},{12,9},{13,... | collective-permute-start | bytes 589832 | tf_op jit(solution)/shard_map/ppermute | solution.py:82
  28.4 28.9 %collective-permute-start.31 = (bf16[96,1024]{1,0:T(8,128)(2,1)}, bf16[96,1024]{1,0:T(8,128)(2,1)}, u32[]{:S(2)}, u32[]{:S(2)}) collective-permute-start(bf16[96,1024]{1,0:T(8,128)(2,1)} %param.15), channel_id=1, source_target_pairs={{4,0},{5,1},{6,2},{7,3},{0,4},{1,5},{2,6},{3,7},{12,8},{13,9},{14,... | collective-permute-start | bytes 589832 | tf_op jit(solution)/shard_map/ppermute | solution.py:82
  30.0 27.4 %collective-permute-start.32 = (bf16[96,1024]{1,0:T(8,128)(2,1)}, bf16[96,1024]{1,0:T(8,128)(2,1)}, u32[]{:S(2)}, u32[]{:S(2)}) collective-permute-start(bf16[96,1024]{1,0:T(8,128)(2,1)} %param.15), channel_id=1, source_target_pairs={{5,0},{6,1},{7,2},{0,3},{1,4},{2,5},{3,6},{4,7},{13,8},{14,9},{15,... | collective-permute-start | bytes 589832 | tf_op jit(solution)/shard_map/ppermute | solution.py:82
  57.3 22.9 %collective-permute-start.10 = (bf16[96,1024]{1,0:T(8,128)(2,1)S(1)}, bf16[96,1024]{1,0:T(8,128)(2,1)S(1)}, u32[]{:S(2)}, u32[]{:S(2)}) collective-permute-start(bf16[96,1024]{1,0:T(8,128)(2,1)S(1)} %get-tuple-element.78), channel_id=1, source_target_pairs={{0,4},{1,5},{2,6},{3,7},{4,0},{5,1},{6,2},{7,3},{8,12},{9,13},{10,... | collective-permute-start | bytes 589832 | tf_op jit(solution)/shard_map/ppermute | solution.py:91
  57.4 22.8 %collective-permute-start.9 = (bf16[96,1024]{1,0:T(8,128)(2,1)S(1)}, bf16[96,1024]{1,0:T(8,128)(2,1)S(1)}, u32[]{:S(2)}, u32[]{:S(2)}) collective-permute-start(bf16[96,1024]{1,0:T(8,128)(2,1)S(1)} %get-tuple-element.79), channel_id=1, source_target_pairs={{0,3},{1,4},{2,5},{3,6},{4,7},{5,0},{6,1},{7,2},{8,11},{9,12},{10,... | collective-permute-start | bytes 589832 | tf_op jit(solution)/shard_map/ppermute | solution.py:91
  119.4 20.5 %collective-permute-start.37 = (bf16[96,1024]{1,0:T(8,128)(2,1)S(1)}, bf16[96,1024]{1,0:T(8,128)(2,1)S(1)}, u32[]{:S(2)}, u32[]{:S(2)}) collective-permute-start(bf16[96,1024]{1,0:T(8,128)(2,1)S(1)} %get-tuple-element.65), channel_id=1, source_target_pairs={{0,3},{1,4},{2,5},{3,6},{4,7},{5,0},{6,1},{7,2},{8,11},{9,12},{10,... | collective-permute-start | bytes 589832 | tf_op jit(solution)/shard_map/ppermute | solution.py:91
  149.4 50.9 %collective-permute-start.96 = (bf16[512,512]{1,0:T(8,128)(2,1)S(1)}, bf16[512,512]{1,0:T(8,128)(2,1)S(1)}, u32[]{:S(2)}, u32[]{:S(2)}) collective-permute-start(bf16[512,512]{1,0:T(8,128)(2,1)S(1)} %dynamic-slice_bitcast_fusion.2), channel_id=1, source_target_pairs={{0,8},{8,0},{16,24},{24,16},{32,40},{40,32},{48,56},{56,48},{64,72... | collective-permute-start | bytes 1572872 | tf_op jit(solution)/shard_map/ppermute | solution.py:129
  149.5 53.7 %collective-permute-start.106 = (bf16[512,512]{1,0:T(8,128)(2,1)S(1)}, bf16[512,512]{1,0:T(8,128)(2,1)S(1)}, u32[]{:S(2)}, u32[]{:S(2)}) collective-permute-start(bf16[512,512]{1,0:T(8,128)(2,1)S(1)} %dynamic-slice_bitcast_fusion.1), channel_id=1, source_target_pairs={{0,8},{8,0},{16,24},{24,16},{32,40},{40,32},{48,56},{56,48},{64,72... | collective-permute-start | bytes 1572872 | tf_op jit(solution)/shard_map/ppermute | solution.py:129
  150.0 57.5 %collective-permute-start.116 = (bf16[256,1024]{1,0:T(8,128)(2,1)S(1)}, bf16[256,1024]{1,0:T(8,128)(2,1)S(1)}, u32[]{:S(2)}, u32[]{:S(2)}) collective-permute-start(bf16[256,1024]{1,0:T(8,128)(2,1)S(1)} %dynamic-slice_bitcast_fusion), channel_id=1, source_target_pairs={{0,8},{8,0},{16,24},{24,16},{32,40},{40,32},{48,56},{56,48},{64,72... | collective-permute-start | bytes 1572872 | tf_op jit(solution)/shard_map/ppermute | solution.py:129
  196.0 60.8 %collective-permute-start.55 = (bf16[96,1024]{1,0:T(8,128)(2,1)S(1)}, bf16[96,1024]{1,0:T(8,128)(2,1)S(1)}, u32[]{:S(2)}, u32[]{:S(2)}) collective-permute-start(bf16[96,1024]{1,0:T(8,128)(2,1)S(1)} %get-tuple-element.54), channel_id=1, source_target_pairs={{0,7},{1,0},{2,1},{3,2},{4,3},{5,4},{6,5},{7,6},{8,15},{9,8},{10,9... | collective-permute-start | bytes 589832 | tf_op jit(solution)/shard_map/ppermute | solution.py:91
  196.3 63.0 %collective-permute-start.54 = (bf16[96,1024]{1,0:T(8,128)(2,1)S(1)}, bf16[96,1024]{1,0:T(8,128)(2,1)S(1)}, u32[]{:S(2)}, u32[]{:S(2)}) collective-permute-start(bf16[96,1024]{1,0:T(8,128)(2,1)S(1)} %get-tuple-element.55), channel_id=1, source_target_pairs={{0,6},{1,7},{2,0},{3,1},{4,2},{5,3},{6,4},{7,5},{8,14},{9,15},{10,... | collective-permute-start | bytes 589832 | tf_op jit(solution)/shard_map/ppermute | solution.py:91
  225.5 33.8 %collective-permute-start.53 = (bf16[96,1024]{1,0:T(8,128)(2,1)S(1)}, bf16[96,1024]{1,0:T(8,128)(2,1)S(1)}, u32[]{:S(2)}, u32[]{:S(2)}) collective-permute-start(bf16[96,1024]{1,0:T(8,128)(2,1)S(1)} %get-tuple-element.56), channel_id=1, source_target_pairs={{0,5},{1,6},{2,7},{3,0},{4,1},{5,2},{6,3},{7,4},{8,13},{9,14},{10,... | collective-permute-start | bytes 589832 | tf_op jit(solution)/shard_map/ppermute | solution.py:91
  229.6 31.4 %collective-permute-start.52 = (bf16[96,1024]{1,0:T(8,128)(2,1)S(1)}, bf16[96,1024]{1,0:T(8,128)(2,1)S(1)}, u32[]{:S(2)}, u32[]{:S(2)}) collective-permute-start(bf16[96,1024]{1,0:T(8,128)(2,1)S(1)} %get-tuple-element.57), channel_id=1, source_target_pairs={{0,4},{1,5},{2,6},{3,7},{4,0},{5,1},{6,2},{7,3},{8,12},{9,13},{10,... | collective-permute-start | bytes 589832 | tf_op jit(solution)/shard_map/ppermute | solution.py:91
  259.3 157.1 %collective-permute-start.99 = (bf16[128,512]{1,0:T(8,128)(2,1)}, bf16[128,512]{1,0:T(8,128)(2,1)S(1)}, u32[]{:S(2)}, u32[]{:S(2)}) collective-permute-start(bf16[128,512]{1,0:T(8,128)(2,1)} %get-tuple-element.88), channel_id=1, source_target_pairs={{0,48},{8,56},{16,0},{24,8},{32,16},{40,24},{48,32},{56,40},{64,11... | collective-permute-start | bytes 393224 | tf_op jit(solution)/shard_map/ppermute | solution.py:135
  260.9 155.6 %collective-permute-start.98 = (bf16[128,512]{1,0:T(8,128)(2,1)}, bf16[128,512]{1,0:T(8,128)(2,1)S(1)}, u32[]{:S(2)}, u32[]{:S(2)}) collective-permute-start(bf16[128,512]{1,0:T(8,128)(2,1)} %get-tuple-element.89), channel_id=1, source_target_pairs={{0,32},{8,40},{16,48},{24,56},{32,0},{40,8},{48,16},{56,24},{64,96... | collective-permute-start | bytes 393224 | tf_op jit(solution)/shard_map/ppermute | solution.py:135
  264.0 155.8 %collective-permute-start.97 = (bf16[128,512]{1,0:T(8,128)(2,1)}, bf16[128,512]{1,0:T(8,128)(2,1)}, u32[]{:S(2)}, u32[]{:S(2)}) collective-permute-start(bf16[128,512]{1,0:T(8,128)(2,1)} %get-tuple-element.87), channel_id=1, source_target_pairs={{0,16},{8,24},{16,32},{24,40},{32,48},{40,56},{48,0},{56,8},{64,80... | collective-permute-start | bytes 393224 | tf_op jit(solution)/shard_map/ppermute | solution.py:135
  265.5 156.4 %collective-permute-start.109 = (bf16[128,512]{1,0:T(8,128)(2,1)}, bf16[128,512]{1,0:T(8,128)(2,1)S(1)}, u32[]{:S(2)}, u32[]{:S(2)}) collective-permute-start(bf16[128,512]{1,0:T(8,128)(2,1)} %get-tuple-element.85), channel_id=1, source_target_pairs={{0,48},{8,56},{16,0},{24,8},{32,16},{40,24},{48,32},{56,40},{64,11... | collective-permute-start | bytes 393224 | tf_op jit(solution)/shard_map/ppermute | solution.py:135
  289.1 65.0 %collective-permute-start.62 = (bf16[128,128]{1,0:T(8,128)(2,1)}, bf16[128,128]{1,0:T(8,128)(2,1)}, u32[]{:S(2)}, u32[]{:S(2)}) collective-permute-start(bf16[128,128]{1,0:T(8,128)(2,1)} %get-tuple-element.38), channel_id=1, source_target_pairs={{16,0},{24,8},{32,16},{40,24},{48,32},{56,40},{0,48},{8,56},{80,64... | collective-permute-start | bytes 98312 | tf_op jit(solution)/shard_map/ppermute | solution.py:149
  422.8 25.5 %collective-permute-start.65 = (bf16[512,128]{1,0:T(8,128)(2,1)S(1)}, bf16[512,128]{1,0:T(8,128)(2,1)S(1)}, u32[]{:S(2)}, u32[]{:S(2)}) collective-permute-start(bf16[512,128]{1,0:T(8,128)(2,1)S(1)} %constant_dynamic-slice_fusion.6), channel_id=1, source_target_pairs={{0,8},{8,0},{16,24},{24,16},{32,40},{40,32},{48,56},{56,48},{64,72... | collective-permute-start | bytes 393224 | tf_op jit(solution)/shard_map/ppermute | solution.py:153
  423.1 29.2 %collective-permute-start.75 = (bf16[512,128]{1,0:T(8,128)(2,1)S(1)}, bf16[512,128]{1,0:T(8,128)(2,1)S(1)}, u32[]{:S(2)}, u32[]{:S(2)}) collective-permute-start(bf16[512,128]{1,0:T(8,128)(2,1)S(1)} %constant_dynamic-slice_fusion.5), channel_id=1, source_target_pairs={{0,8},{8,0},{16,24},{24,16},{32,40},{40,32},{48,56},{56,48},{64,72... | collective-permute-start | bytes 393224 | tf_op jit(solution)/shard_map/ppermute | solution.py:153
  423.4 57.8 %collective-permute-start.85 = (bf16[512,128]{1,0:T(8,128)(2,1)S(1)}, bf16[512,128]{1,0:T(8,128)(2,1)S(1)}, u32[]{:S(2)}, u32[]{:S(2)}) collective-permute-start(bf16[512,128]{1,0:T(8,128)(2,1)S(1)} %constant_dynamic-slice_fusion.4), channel_id=1, source_target_pairs={{0,8},{8,0},{16,24},{24,16},{32,40},{40,32},{48,56},{56,48},{64,72... | collective-permute-start | bytes 393224 | tf_op jit(solution)/shard_map/ppermute | solution.py:153
  426.3 57.5 %collective-permute-start.95 = (bf16[64,1024]{1,0:T(8,128)(2,1)S(1)}, bf16[64,1024]{1,0:T(8,128)(2,1)S(1)}, u32[]{:S(2)}, u32[]{:S(2)}) collective-permute-start(bf16[64,1024]{1,0:T(8,128)(2,1)S(1)} %constant_dynamic-slice_fusion.3), channel_id=1, source_target_pairs={{0,8},{8,0},{16,24},{24,16},{32,40},{40,32},{48,56},{56,48},{64,72... | collective-permute-start | bytes 393224 | tf_op jit(solution)/shard_map/ppermute | solution.py:153
  (136 other events, 1700.8 us)
